TPU v7x, 32 devices: a whole 2x2x4 slice. The times are simulated.
32 devices in a mesh: sta: 16 (over z, x, core), strike: 2 (over y).
Axes of the slice: x: 2, y: 2, z: 4, core: 2. Of those that a mesh axis runs over, the one named last changes fastest.
Arguments:
- data: float32 [128, 512], P('sta'), may hold values from -6 to 6
- model: float32 [64, 64, 128], P(None, 'strike'), may hold values from -6 to 6
- green: bfloat16 [16, 2, 96, 128, 128], P('sta', 'strike'), may hold values from -0.03125 to 0.03125
- block_ids: int32 [16, 2, 96], P('sta', 'strike'), may hold values from -1 to 1023, as said below
Outputs:
- residual: float32 [128, 512], P('sta')
- updated: float32 [64, 64, 128], P(None, 'strike')
Inputs may be any that keep to these rules, and one draw needn't show every extreme that they name: In each block_ids[g, h] the ids that are not -1 are distinct and stand in the first slots; every pair uses at least a third of its 96 slots, and in every draw some pair uses all 96.
All inputs are finite; a program needn't handle non-finite values.
Results may differ from a plain program's by a relative error of at most 0.0023.
Values sent between devices are 32-bit elements; how exact they have to be, the bound alone decides.
A program may use at most 64 MiB of HBM per device.

v0:
```python
import jax
import jax.numpy as jnp
from jax import lax
from jax.sharding import PartitionSpec as P

SWEEPS = 4


NU_DIFF = 0.1
STEP_LEN = 4.0


def extended(block, sides, width):
    for axis, dim in sides:
        count = lax.axis_size(axis)
        forward = [(i, i + 1) for i in range(count - 1)]
        backward = [(target, source) for source, target in forward]
        low = lax.ppermute(
            lax.slice_in_dim(block, block.shape[dim] - width, None, axis=dim), axis, forward
        )
        high = lax.ppermute(lax.slice_in_dim(block, 0, width, axis=dim), axis, backward)
        block = jnp.concatenate([low, block, high], axis=dim)
    return block


def shear_add(series):
    count_rows, windows, length = series.shape
    padded = jnp.pad(series, ((0, 0), (0, 0), (0, windows)))
    flattened = padded.reshape(count_rows, windows * (length + windows))[
        :, : windows * (length + windows - 1)
    ]
    sheared = flattened.reshape(count_rows, windows, length + windows - 1)
    return jnp.sum(sheared[:, :, :length], axis=1)


def shear_take(residual, windows):
    count_rows, length = residual.shape
    padded = jnp.pad(residual, ((0, 0), (0, windows)))
    repeated = jnp.broadcast_to(padded[:, None, :], (count_rows, windows, length + windows))
    repeated = repeated.reshape(count_rows, windows * (length + windows))
    repeated = jnp.pad(repeated, ((0, 0), (0, windows)))
    return repeated.reshape(count_rows, windows, length + windows + 1)[:, :, :length]


def laplace_step(padded, field):
    laplace = (
        padded[:, 2:, 1:-1]
        + padded[:, :-2, 1:-1]
        + padded[:, 1:-1, 2:]
        + padded[:, 1:-1, :-2]
        - 4.0 * field
    )
    return field + NU_DIFF * laplace


def local(data, model, green, block_ids):
    sta_rows, samples = data.shape
    windows, strike_rows, dip_cells = model.shape
    block = green.shape[-1]
    time_blocks = samples // block
    row_count = sta_rows * time_blocks
    blocks = green.reshape(green.shape[2:])
    slot_ids = block_ids.reshape(-1)
    usable = slot_ids >= 0
    safe_ids = jnp.where(usable, slot_ids, 0)
    row_block = safe_ids // strike_rows
    col_block = safe_ids % strike_rows
    row_target = jnp.where(usable, row_block, row_count)
    col_target = jnp.where(usable, col_block, strike_rows)
    model_bf = model.astype(jnp.bfloat16)
    columns = jnp.take(model_bf, col_block, axis=1)
    products = jnp.einsum("cts,wcs->cwt", blocks, columns, preferred_element_type=jnp.float32)
    gathered = jax.ops.segment_sum(products, row_target, num_segments=row_count)
    series = (
        gathered.reshape(sta_rows, time_blocks, windows, block)
        .transpose(0, 2, 1, 3)
        .reshape(sta_rows, windows, samples)
    )
    partial_synth = shear_add(series)
    residual = lax.psum(partial_synth, "strike") - data
    resid_bf = residual.astype(jnp.bfloat16)
    shifted = shear_take(resid_bf, windows)
    row_blocks = (
        shifted.reshape(sta_rows, windows, time_blocks, block)
        .transpose(0, 2, 1, 3)
        .reshape(row_count, windows, block)
    )
    res_rows = jnp.take(row_blocks, row_block, axis=0)
    slot_grads = jnp.einsum("cts,cwt->cws", blocks, res_rows, preferred_element_type=jnp.float32)
    per_patch = jax.ops.segment_sum(slot_grads, col_target, num_segments=strike_rows)
    partial_grad = per_patch.transpose(1, 0, 2)
    field = lax.psum(partial_grad, "sta")
    for sweep in range(SWEEPS):
        padded = extended(field, (("strike", 1),), 1)
        padded = jnp.pad(padded, ((0, 0), (0, 0), (1, 1)))
        field = laplace_step(padded, field)
    updated = model - STEP_LEN * field
    return (residual, updated)


def solution(mesh):
    in_specs = (
        P("sta", None),
        P(None, "strike", None),
        P("sta", "strike", None, None, None),
        P("sta", "strike", None),
    )
    out_specs = (P("sta", None), P(None, "strike", None))
    return jax.shard_map(local, mesh=mesh, in_specs=in_specs, out_specs=out_specs, check_vma=False)
```

profile of v0, /device:TPU:0, one launch (start us, length us, event | category | flops | bytes accessed | tf_op | source)
XLA Modules:
  0.0 228.9 jit_solution(13629013439439119440)
XLA Ops:
  7.2 0.0 copy-start
  7.2 0.0 all-reduce.9.cloned.1.call-start
  7.2 0.8 fusion.33
  8.0 0.8 compare_and_fusion
  8.8 0.7 fusion.31
  9.5 2.6 %copy.16 = bf16[64,32,128]{2,0,1:T(8,128)(2,1)} copy(f32[64,32,128]{2,1,0:T(8,128)} %param.5) | data formatting | bytes 1572864 | tf_op args[1]
  12.1 3.0 %gather_fusion = bf16[96,64,128]{2,1,0:T(8,128)(2,1)} fusion(bf16[64,32,128]{2,0,1:T(8,128)(2,1)} %copy.16, s32[1024]{0:T(1024)S(1)} %pad_clamp_fusion.1), kind=kCustom, calls=%fused_computation | custom fusion | bytes 3146112 | tf_op jit(solution)/shard_map/jit(_take)/gather | solution.py:71
  15.1 0.0 copy-done
  15.1 5.3 %fusion.2 = f32[96,64,128]{2,1,0:T(8,128)} fusion(bf16[1,1,96,128,128]{4,3,2,1,0:T(8,128)(2,1)S(1)} %copy-done, bf16[96,64,128]{2,1,0:T(8,128)(2,1)} %gather_fusion, pred[96]{0:T(512)(128)(4,1)S(1)} %compare_and_fusion.1), kind=kOutput, calls=%fused_computation.8 | convolution fusion | flops 202113024 | bytes 7864416 | tf_op jit(solution)/shard_map/cts,wcs->cwt/dot_general | solution.py:72
  20.4 1.1 broadcast.280.clone
  21.5 15.1 %scatter_fusion = f32[32,64,128]{2,1,0:T(8,128)} fusion(f32[32,64,128]{2,1,0:T(8,128)} %broadcast.280.clone, s32[96]{0:T(128)S(1)} %get-tuple-element.25, f32[96,64,128]{2,1,0:T(8,128)} %fusion.2), kind=kCustom, calls=%fused_computation.2 | custom fusion | flops 786432 | bytes 9437568 | tf_op jit(solution)/shard_map/scatter-add | solution.py:73
  36.5 1.3 copy.17
  37.9 1.2 pad.25
  39.1 2.9 %reshape.180 = f32[8,36864]{1,0:T(8,128)} reshape(f32[8,64,576]{2,1,0:T(8,128)} %pad.25) | data formatting | bytes 2359296 | tf_op jit(solution)/shard_map/reshape | solution.py:29
  42.0 0.0 copy-start.3
  42.0 3.6 %reshape.181 = f32[8,64,575]{2,1,0:T(8,128)} reshape(f32[8,36800]{1,0:T(8,128)} %bitcast.46) | data formatting | bytes 2355200 | tf_op jit(solution)/shard_map/reshape | solution.py:32
  45.6 1.3 slice_reduce_fusion
  47.0 8.7 %psum.14 = f32[8,512]{1,0:T(8,128)S(1)} all-reduce(f32[8,512]{1,0:T(8,128)S(1)} %slice_reduce_fusion), channel_id=1, replica_groups=mesh['sta'=16,'strike'=2] {'strike'}, use_global_device_ids=true, to_apply=%region_2.3 | all-reduce | flops 4096 | bytes 32768 | tf_op jit(solution)/shard_map/psum | solution.py:80
  55.7 0.0 copy-done.3
  55.7 0.6 fusion.36
  56.3 0.9 broadcast_in_dim.35
  57.2 2.7 %reshape.182 = bf16[8,36864]{1,0:T(8,128)(2,1)} reshape(bf16[8,64,576]{2,1,0:T(8,128)(2,1)} %broadcast_in_dim.35) | data formatting | bytes 1179648 | tf_op jit(solution)/shard_map/reshape | solution.py:40
  59.9 1.9 pad.27
  61.8 3.3 %reshape.183 = bf16[8,64,577]{2,1,0:T(8,128)(2,1)} reshape(bf16[8,36928]{1,0:T(8,128)(2,1)} %pad.27) | data formatting | bytes 1181696 | tf_op jit(solution)/shard_map/reshape | solution.py:42
  65.1 1.1 fusion.41
  66.2 0.8 pad_maximum_fusion.8
  67.1 3.0 %gather_fusion.1 = bf16[96,64,128]{2,1,0:T(8,128)(2,1)} fusion(bf16[32,64,128]{2,1,0:T(8,128)(2,1)} %bitcast.45, s32[1024]{0:T(1024)S(1)} %pad_clamp_fusion), kind=kCustom, calls=%fused_computation.1 | custom fusion | bytes 3146112 | tf_op jit(solution)/shard_map/jit(_take)/gather | solution.py:88
  70.1 4.0 %fusion = f32[96,64,128]{2,1,0:T(8,128)} fusion(bf16[1,1,96,128,128]{4,3,2,1,0:T(8,128)(2,1)S(1)} %copy-done, bf16[96,64,128]{2,1,0:T(8,128)(2,1)} %gather_fusion.1, pred[96]{0:T(512)(128)(4,1)S(1)} %get-tuple-element.4), kind=kOutput, calls=%fused_computation.6 | convolution fusion | flops 202113024 | bytes 7864416 | tf_op jit(solution)/shard_map/cts,cwt->cws/dot_general | solution.py:89
  74.1 1.1 broadcast.280
  75.2 15.1 %scatter_fusion.1 = f32[32,64,128]{2,1,0:T(8,128)} fusion(f32[32,64,128]{2,1,0:T(8,128)} %broadcast.280, s32[96]{0:T(128)S(1)} %get-tuple-element.23, f32[96,64,128]{2,1,0:T(8,128)} %fusion), kind=kCustom, calls=%fused_computation.3 | custom fusion | flops 786432 | bytes 9437568 | tf_op jit(solution)/shard_map/scatter-add | solution.py:90
  90.3 0.0 all-reduce.9.cloned.1.call-update
  90.3 93.6 %all-reduce.9.cloned.1.call-done = f32[64,32,128]{2,0,1:T(8,128)} async-done(((f32[64,32,128]{2,0,1:T(8,128)}), f32[64,32,128]{2,0,1:T(8,128)}) %all-reduce.9.cloned.1.call-update) | async-done | bytes 1048592 | tf_op jit(solution)/shard_map/psum | solution.py:92
  183.9 0.0 copy-start.1
  183.9 0.9 fusion.40
  184.8 1.3 collective-permute-start
  186.1 4.5 %collective-permute-start.1 = (f32[64,1,128]{2,0,1:T(8,128)S(1)}, f32[64,1,128]{2,0,1:T(8,128)S(1)}, u32[]{:S(2)}, u32[]{:S(2)}) collective-permute-start(f32[64,1,128]{2,0,1:T(8,128)S(1)} %get-tuple-element.17), channel_id=1, source_target_pairs={{0,1},{2,3},{4,5},{6,7},{8,9},{10,11},{12,13},{14,15},{16,17},{18,... | collective-permute-start | bytes 98312 | tf_op jit(solution)/shard_map/ppermute | solution.py:18
  190.6 0.0 collective-permute-done
  190.6 1.6 collective-permute-done.1
  192.2 1.9 select_maximum_fusion.6
  194.1 0.0 copy-done.1
  194.1 0.4 fusion.26
  194.5 1.3 collective-permute-start.2
  195.8 4.5 %collective-permute-start.3 = (f32[64,1,128]{2,0,1:T(8,128)S(1)}, f32[64,1,128]{2,0,1:T(8,128)S(1)}, u32[]{:S(2)}, u32[]{:S(2)}) collective-permute-start(f32[64,1,128]{2,0,1:T(8,128)S(1)} %get-tuple-element.15), channel_id=1, source_target_pairs={{0,1},{2,3},{4,5},{6,7},{8,9},{10,11},{12,13},{14,15},{16,17},{18,... | collective-permute-start | bytes 98312 | tf_op jit(solution)/shard_map/ppermute | solution.py:18
  200.3 0.0 collective-permute-done.2
  200.3 1.6 collective-permute-done.3
  201.9 0.6 select_maximum_fusion.4
  202.5 0.4 fusion.22
  202.9 1.3 collective-permute-start.4
  204.2 4.7 %collective-permute-start.5 = (f32[64,1,128]{2,0,1:T(8,128)S(1)}, f32[64,1,128]{2,0,1:T(8,128)S(1)}, u32[]{:S(2)}, u32[]{:S(2)}) collective-permute-start(f32[64,1,128]{2,0,1:T(8,128)S(1)} %get-tuple-element.13), channel_id=1, source_target_pairs={{0,1},{2,3},{4,5},{6,7},{8,9},{10,11},{12,13},{14,15},{16,17},{18,... | collective-permute-start | bytes 98312 | tf_op jit(solution)/shard_map/ppermute | solution.py:18
  208.9 0.0 collective-permute-done.4
  209.0 1.4 collective-permute-done.5
  210.3 0.6 select_maximum_fusion.2
  211.0 0.4 fusion.18
  211.4 0.0 copy-start.2
  211.4 1.4 collective-permute-start.6
  212.8 4.5 %collective-permute-start.7 = (f32[64,1,128]{2,0,1:T(8,128)S(1)}, f32[64,1,128]{2,0,1:T(8,128)S(1)}, u32[]{:S(2)}, u32[]{:S(2)}) collective-permute-start(f32[64,1,128]{2,0,1:T(8,128)S(1)} %get-tuple-element.11), channel_id=1, source_target_pairs={{0,1},{2,3},{4,5},{6,7},{8,9},{10,11},{12,13},{14,15},{16,17},{18,... | collective-permute-start | bytes 98312 | tf_op jit(solution)/shard_map/ppermute | solution.py:18
  217.4 0.0 collective-permute-done.6
  217.4 1.6 collective-permute-done.7
  218.9 0.6 select_maximum_fusion
  219.6 0.0 copy-done.2
  219.6 0.9 fusion.14
  220.5 1.6 copy.11
  (7 shorter events, 0.0 us)
Async XLA Ops:
  7.2 8.0 %copy-start = (bf16[1,1,96,128,128]{4,3,2,1,0:T(8,128)(2,1)S(1)}, bf16[1,1,96,128,128]{4,3,2,1,0:T(8,128)(2,1)}, u32[]{:S(2)}) copy-start(bf16[1,1,96,128,128]{4,3,2,1,0:T(8,128)(2,1)} %param.6) | copy-start | bytes 9437188
  7.2 176.7 %all-reduce.9.cloned.1.call-start = ((), (), s32[]{:S(2)}) async-start(), calls=%async_computation | async-start | bytes 2097152 | tf_op jit(solution)/shard_map/psum | solution.py:92
  42.0 13.6 %copy-start.3 = (f32[8,512]{1,0:T(8,128)S(1)}, f32[8,512]{1,0:T(8,128)}, u32[]{:S(2)}) copy-start(f32[8,512]{1,0:T(8,128)} %param.4) | copy-start | bytes 49156
  183.9 10.2 %copy-start.1 = (f32[64,32,128]{2,0,1:T(8,128)S(1)}, f32[64,32,128]{2,0,1:T(8,128)}, u32[]{:S(2)}) copy-start(f32[64,32,128]{2,0,1:T(8,128)} %all-reduce.9.cloned.1.call-done) | copy-start | bytes 3145732
  184.8 5.8 %collective-permute-start = (f32[64,1,128]{2,0,1:T(8,128)S(1)}, f32[64,1,128]{2,0,1:T(8,128)S(1)}, u32[]{:S(2)}, u32[]{:S(2)}) collective-permute-start(f32[64,1,128]{2,0,1:T(8,128)S(1)} %get-tuple-element.18), channel_id=1, source_target_pairs={{1,0},{3,2},{5,4},{7,6},{9,8},{11,10},{13,12},{15,14},{17,16},{19,... | collective-permute-start | bytes 98312 | tf_op jit(solution)/shard_map/ppermute | solution.py:21
  186.1 6.1 %collective-permute-start.1 = (f32[64,1,128]{2,0,1:T(8,128)S(1)}, f32[64,1,128]{2,0,1:T(8,128)S(1)}, u32[]{:S(2)}, u32[]{:S(2)}) collective-permute-start(f32[64,1,128]{2,0,1:T(8,128)S(1)} %get-tuple-element.17), channel_id=1, source_target_pairs={{0,1},{2,3},{4,5},{6,7},{8,9},{10,11},{12,13},{14,15},{16,17},{18,... | collective-permute-start | bytes 98312 | tf_op jit(solution)/shard_map/ppermute | solution.py:18
  194.5 5.9 %collective-permute-start.2 = (f32[64,1,128]{2,0,1:T(8,128)S(1)}, f32[64,1,128]{2,0,1:T(8,128)S(1)}, u32[]{:S(2)}, u32[]{:S(2)}) collective-permute-start(f32[64,1,128]{2,0,1:T(8,128)S(1)} %get-tuple-element.16), channel_id=1, source_target_pairs={{1,0},{3,2},{5,4},{7,6},{9,8},{11,10},{13,12},{15,14},{17,16},{19,... | collective-permute-start | bytes 98312 | tf_op jit(solution)/shard_map/ppermute | solution.py:21
  195.8 6.1 %collective-permute-start.3 = (f32[64,1,128]{2,0,1:T(8,128)S(1)}, f32[64,1,128]{2,0,1:T(8,128)S(1)}, u32[]{:S(2)}, u32[]{:S(2)}) collective-permute-start(f32[64,1,128]{2,0,1:T(8,128)S(1)} %get-tuple-element.15), channel_id=1, source_target_pairs={{0,1},{2,3},{4,5},{6,7},{8,9},{10,11},{12,13},{14,15},{16,17},{18,... | collective-permute-start | bytes 98312 | tf_op jit(solution)/shard_map/ppermute | solution.py:18
  202.9 6.0 %collective-permute-start.4 = (f32[64,1,128]{2,0,1:T(8,128)S(1)}, f32[64,1,128]{2,0,1:T(8,128)S(1)}, u32[]{:S(2)}, u32[]{:S(2)}) collective-permute-start(f32[64,1,128]{2,0,1:T(8,128)S(1)} %get-tuple-element.14), channel_id=1, source_target_pairs={{1,0},{3,2},{5,4},{7,6},{9,8},{11,10},{13,12},{15,14},{17,16},{19,... | collective-permute-start | bytes 98312 | tf_op jit(solution)/shard_map/ppermute | solution.py:21
  204.2 6.1 %collective-permute-start.5 = (f32[64,1,128]{2,0,1:T(8,128)S(1)}, f32[64,1,128]{2,0,1:T(8,128)S(1)}, u32[]{:S(2)}, u32[]{:S(2)}) collective-permute-start(f32[64,1,128]{2,0,1:T(8,128)S(1)} %get-tuple-element.13), channel_id=1, source_target_pairs={{0,1},{2,3},{4,5},{6,7},{8,9},{10,11},{12,13},{14,15},{16,17},{18,... | collective-permute-start | bytes 98312 | tf_op jit(solution)/shard_map/ppermute | solution.py:18
  211.4 8.2 %copy-start.2 = (f32[64,32,128]{2,1,0:T(8,128)S(1)}, f32[64,32,128]{2,1,0:T(8,128)}, u32[]{:S(2)}) copy-start(f32[64,32,128]{2,1,0:T(8,128)} %param.5) | copy-start | bytes 3145732
  211.4 6.0 %collective-permute-start.6 = (f32[64,1,128]{2,0,1:T(8,128)S(1)}, f32[64,1,128]{2,0,1:T(8,128)S(1)}, u32[]{:S(2)}, u32[]{:S(2)}) collective-permute-start(f32[64,1,128]{2,0,1:T(8,128)S(1)} %get-tuple-element.12), channel_id=1, source_target_pairs={{1,0},{3,2},{5,4},{7,6},{9,8},{11,10},{13,12},{15,14},{17,16},{19,... | collective-permute-start | bytes 98312 | tf_op jit(solution)/shard_map/ppermute | solution.py:21
  212.8 6.1 %collective-permute-start.7 = (f32[64,1,128]{2,0,1:T(8,128)S(1)}, f32[64,1,128]{2,0,1:T(8,128)S(1)}, u32[]{:S(2)}, u32[]{:S(2)}) collective-permute-start(f32[64,1,128]{2,0,1:T(8,128)S(1)} %get-tuple-element.11), channel_id=1, source_target_pairs={{0,1},{2,3},{4,5},{6,7},{8,9},{10,11},{12,13},{14,15},{16,17},{18,... | collective-permute-start | bytes 98312 | tf_op jit(solution)/shard_map/ppermute | solution.py:18
Sparse Core Ops, SparseCore 0:
  90.4 93.4 all-reduce.8
where the time goes:
time: 230 us; the launch traced here: 229 us
  waiting for transfers between devices  99.7 us (43%)
  other arithmetic  40.9 us (18%)
  local copies, waits for them, and re-layouts  32.3 us (14%)
  starting transfers between devices  23.7 us (10%)
  between operations  14.3 us (6%)
  matrix products  9.33 us (4%)
  blocking collectives  8.7 us (4%)
    psum x1, waiting for transfers between devices, local(): field = lax.psum(partial_grad, 'sta')  93.6 us
    ppermute x4, starting transfers between devices, extended(): lax.ppermute(lax.slice_in_dim(block, block.shape[dim] - width, None, axis...  18.4 us
    scatter-add x1, other arithmetic, local(): jax.ops.segment_sum(slot_grads, col_target, num_segments=strike_rows)  15.1 us
    scatter-add x1, other arithmetic, local(): gathered = jax.ops.segment_sum(products, row_target, num_segments=row_count)  15.1 us
    psum x1, blocking collectives, local(): residual = lax.psum(partial_synth, 'strike') - data  8.7 us
    ppermute x4, waiting for transfers between devices, extended(): lax.ppermute(lax.slice_in_dim(block, block.shape[dim] - width, None, axis...  6.09 us
    ppermute x4, starting transfers between devices, extended(): lax.ppermute(lax.slice_in_dim(block, 0, width, axis=dim), axis, backward)  5.29 us
    dot_general x1, matrix products, local(): jnp.einsum('cts,wcs->cwt', blocks, columns, preferred_element_type=jnp.fl...  5.28 us
  transfers between devices with their start and end apart: 9, of which 5 were waited for; matrix products, arithmetic and copies ran while one was open for 0% of the time, Pallas kernels for 0%

commit v1 on v0

v1 whole, which is shorter than its diff:
```python
import functools

import jax
import jax.numpy as jnp
from jax import lax
from jax.experimental import pallas as pl
from jax.experimental.pallas import tpu as pltpu
from jax.sharding import PartitionSpec as P

SWEEPS = 4
NU_DIFF = 0.1
STEP_LEN = 4.0
MESH = pl.DeviceIdType.MESH
CHUNKS = 6
HALO = 8


def green_copy(green_ref, gbuf, sems, i, size):
    return pltpu.make_async_copy(
        green_ref.at[pl.ds(i * size, size)], gbuf.at[pl.ds(i * size, size)], sems.at[i]
    )


def forward_kernel(strike_rows, ids_ref, model_ref, green_ref, out_ref, gbuf, cols, prod, acc, sems):
    slots, block = gbuf.shape[:2]
    windows = cols.shape[1]
    sta_rows, samples = out_ref.shape
    time_blocks = samples // block
    row_count = sta_rows * time_blocks
    size = slots // CHUNKS
    for i in range(CHUNKS):
        green_copy(green_ref, gbuf, sems, i, size).start()
    acc[...] = jnp.zeros_like(acc)
    for q in range(strike_rows):
        cols[q] = model_ref[pl.ds(q, windows, stride=strike_rows), :].astype(jnp.bfloat16)

    @pl.loop(0, CHUNKS)
    def _(i):
        green_copy(green_ref, gbuf, sems, i, size).wait()
        for u in range(size):
            c = i * size + u
            q = lax.rem(jnp.maximum(ids_ref[c], 0), strike_rows)
            prod[c] = lax.dot_general(
                cols[q], gbuf[c], (((1,), (1,)), ((), ())), preferred_element_type=jnp.float32
            )

    @pl.loop(0, slots, step=4)
    def _(base):
        for u in range(4):
            slot_id = ids_ref[base + u]
            row = jnp.where(slot_id >= 0, lax.div(jnp.maximum(slot_id, 0), strike_rows), row_count)
            acc[row] = acc[row] + prod[base + u]

    window = lax.broadcasted_iota(jnp.int32, (windows, block), 0)
    lane = lax.broadcasted_iota(jnp.int32, (windows, block), 1)
    same = lane >= window
    for a in range(sta_rows):
        before = jnp.zeros((windows, block), jnp.float32)
        for b in range(time_blocks):
            rolled = pltpu.roll(acc[a * time_blocks + b], 0, 1, stride=1, stride_axis=0)
            out_ref[a : a + 1, b * block : (b + 1) * block] = jnp.sum(
                jnp.where(same, rolled, before), axis=0, keepdims=True
            )
            before = rolled


def adjoint_kernel(strike_rows, ids_ref, resid_ref, green_ref, out_ref, gbuf, rows, prod, acc, sems):
    slots, block = gbuf.shape[:2]
    windows = rows.shape[1]
    sta_rows, samples = resid_ref.shape
    time_blocks = samples // block
    size = slots // CHUNKS
    for i in range(CHUNKS):
        green_copy(green_ref, gbuf, sems, i, size).start()
    acc[...] = jnp.zeros_like(acc)
    back = windows - 1 - lax.broadcasted_iota(jnp.int32, (windows, block), 0)
    same = lax.broadcasted_iota(jnp.int32, (windows, block), 1) + back < block
    for a in range(sta_rows):
        after = jnp.zeros((windows, block), jnp.float32)
        for b in reversed(range(time_blocks)):
            line = jnp.broadcast_to(resid_ref[a : a + 1, b * block : (b + 1) * block], (windows, block))
            rolled = pltpu.roll(line, block - windows + 1, 1, stride=1, stride_axis=0)
            rows[a * time_blocks + b] = jnp.where(same, rolled, after).astype(jnp.bfloat16)
            after = rolled

    @pl.loop(0, CHUNKS)
    def _(i):
        green_copy(green_ref, gbuf, sems, i, size).wait()
        for u in range(size):
            c = i * size + u
            row = lax.div(jnp.maximum(ids_ref[c], 0), strike_rows)
            prod[c] = jnp.dot(rows[row], gbuf[c], preferred_element_type=jnp.float32)

    @pl.loop(0, slots, step=4)
    def _(base):
        for u in range(4):
            slot_id = ids_ref[base + u]
            q = jnp.where(slot_id >= 0, lax.rem(jnp.maximum(slot_id, 0), strike_rows), strike_rows)
            here = pl.ds(pl.multiple_of(q * windows, windows), windows)
            acc[here, :] = acc[here, :] + prod[base + u]

    for w in range(windows):
        out_ref[w * strike_rows : (w + 1) * strike_rows, :] = acc[
            pl.ds(windows - 1 - w, strike_rows, stride=windows), :
        ]


def exchange_kernel(n, part_ref, data_ref, out_ref, parts, send, recv):
    me = lax.axis_index("strike")
    barrier = pltpu.get_barrier_semaphore()
    for d in range(1, n):
        pl.semaphore_signal(
            barrier, inc=1, device_id={"strike": lax.rem(me + d, n)}, device_id_type=MESH
        )
    pl.semaphore_wait(barrier, n - 1)
    copies = []
    for d in range(1, n):
        copy = pltpu.make_async_remote_copy(
            src_ref=part_ref,
            dst_ref=parts.at[d],
            send_sem=send.at[d],
            recv_sem=recv.at[d],
            device_id={"strike": lax.rem(me + d, n)},
            device_id_type=MESH,
        )
        copy.start()
        copies.append(copy)
    parts[0] = part_ref[...]
    for copy in copies:
        copy.wait()
    total = parts[lax.rem(me, n)]
    for j in range(1, n):
        total = total + parts[lax.rem(me - j + n, n)]
    out_ref[...] = total - data_ref[...]


def reduce_kernel(
    n_sta, n_strike, pieces, grad_ref, model_ref, out_ref, from_core, from_x, from_z, ext,
    core_s, core_r, x_s, x_r, z_s, z_r, halo_s, halo_r, gz_s, gz_r, gx_s, gx_r, gc_s, gc_r,
):
    depth = n_sta // 4
    own = grad_ref.shape[3]
    rows, dip = grad_ref.shape[4:]
    part = own // pieces
    sta = lax.axis_index("sta")
    strike = lax.axis_index("strike")
    core = lax.rem(sta, 2)
    x = lax.rem(lax.div(sta, 2), 2)
    z = lax.div(sta, 4)
    other_core, other_x = 1 - core, 1 - x
    core_dev = {"sta": z * 4 + x * 2 + other_core}
    x_dev = {"sta": z * 4 + other_x * 2 + core}

    def z_at(d):
        return lax.rem(z + d, depth)

    def z_dev(d):
        return {"sta": z_at(d) * 4 + x * 2 + core}

    up_dev = {"strike": lax.rem(strike + 1, n_strike)}
    down_dev = {"strike": lax.rem(strike + n_strike - 1, n_strike)}
    peers = [core_dev, x_dev] + [z_dev(d) for d in range(1, depth)] + [up_dev, down_dev]
    barrier = pltpu.get_barrier_semaphore()
    for peer in peers:
        pl.semaphore_signal(barrier, inc=1, device_id=peer, device_id_type=MESH)
    pl.semaphore_wait(barrier, len(peers))

    started = []

    def send(src, dst, s, r, dev):
        copy = pltpu.make_async_remote_copy(
            src_ref=src, dst_ref=dst, send_sem=s, recv_sem=r, device_id=dev, device_id_type=MESH
        )
        copy.start()
        started.append(copy)
        return copy

    def cut(k):
        return pl.ds(k * part, part)

    halves = []
    for h, side in enumerate((other_x, x)):
        for k in range(pieces):
            halves.append(
                send(
                    grad_ref.at[other_core, side, :, cut(k)],
                    from_core.at[h, :, cut(k)],
                    core_s.at[h, k],
                    core_r.at[h, k],
                    core_dev,
                )
            )
    across = []
    for k in range(pieces):
        halves[k].wait_recv()
        from_core[0, :, cut(k)] = from_core[0, :, cut(k)] + grad_ref[core, other_x, :, cut(k)]
        across.append(
            send(from_core.at[0, :, cut(k)], from_x.at[:, cut(k)], x_s.at[k], x_r.at[k], x_dev)
        )
    for k in range(pieces):
        halves[pieces + k].wait_recv()
        from_core[1, :, cut(k)] = from_core[1, :, cut(k)] + grad_ref[core, x, :, cut(k)]
    along = []
    for k in range(pieces):
        across[k].wait_recv()
        from_x[:, cut(k)] = from_x[:, cut(k)] + from_core[1, :, cut(k)]
        for d in range(1, depth):
            along.append(
                send(
                    from_x.at[z_at(d), cut(k)],
                    from_z.at[d - 1, cut(k)],
                    z_s.at[d - 1, k],
                    z_r.at[d - 1, k],
                    z_dev(d),
                )
            )
    for copy in along:
        copy.wait_recv()
    field = from_x[z]
    for d in range(1, depth):
        field = field + from_z[d - 1]

    ext[:, HALO : HALO + rows] = field
    high = send(
        ext.at[:, pl.ds(rows, HALO)], ext.at[:, pl.ds(0, HALO)], halo_s.at[0], halo_r.at[0], up_dev
    )
    low = send(
        ext.at[:, pl.ds(HALO, HALO)],
        ext.at[:, pl.ds(HALO + rows, HALO)],
        halo_s.at[1],
        halo_r.at[1],
        down_dev,
    )
    tall = rows + 2 * HALO
    row = lax.broadcasted_iota(jnp.int32, (own, tall, dip), 1)
    lane = lax.broadcasted_iota(jnp.int32, (own, tall, dip), 2)
    first = jnp.where(strike > 0, 0, HALO)
    last = jnp.where(strike < n_strike - 1, tall, HALO + rows)
    inside = (row >= first) & (row < last)
    high.wait_recv()
    low.wait_recv()
    v = jnp.where(inside, ext[...], 0.0)
    for _ in range(SWEEPS):
        left = jnp.where(lane > 0, pltpu.roll(v, 1, 2), 0.0)
        right = jnp.where(lane < dip - 1, pltpu.roll(v, dip - 1, 2), 0.0)
        around = pltpu.roll(v, tall - 1, 1) + pltpu.roll(v, 1, 1) + right + left - 4.0 * v
        v = jnp.where(inside, v + NU_DIFF * around, 0.0)
    out_ref[core, x, z] = model_ref[core, x, z] - STEP_LEN * v[:, HALO : HALO + rows]

    mine = out_ref.at[core, x, z]
    fetched = [send(mine, mine, gz_s.at[d], gz_r.at[d], z_dev(d)) for d in range(1, depth)]
    crossed = []
    to_core = []
    for d in range(depth):
        if d:
            fetched[d - 1].wait_recv()
        block = out_ref.at[core, x, lax.rem(z - d + depth, depth)]
        crossed.append(send(block, block, gx_s.at[d], gx_r.at[d], x_dev))
        to_core.append(send(block, block, gc_s.at[0, d], gc_r.at[0, d], core_dev))
    for d in range(depth):
        crossed[d].wait_recv()
        block = out_ref.at[core, other_x, lax.rem(z - d + depth, depth)]
        to_core.append(send(block, block, gc_s.at[1, d], gc_r.at[1, d], core_dev))
    for copy in to_core:
        copy.wait_recv()
    for copy in started:
        copy.wait_send()


def local(n_sta, n_strike, data, model, green, block_ids):
    sta_rows, samples = data.shape
    windows, strike_rows, dip = model.shape
    slots, block = green.shape[2], green.shape[3]
    row_count = sta_rows * (samples // block)
    green = green.reshape(green.shape[2:])
    ids = block_ids.reshape(-1)
    vmem = pl.BlockSpec(memory_space=pltpu.VMEM)
    smem = pl.BlockSpec(memory_space=pltpu.SMEM)
    hbm = pl.BlockSpec(memory_space=pl.ANY)
    f32 = jnp.float32
    dma = pltpu.SemaphoreType.DMA

    partial = pl.pallas_call(
        functools.partial(forward_kernel, strike_rows),
        out_shape=jax.ShapeDtypeStruct((sta_rows, samples), f32),
        in_specs=[smem, vmem, hbm],
        out_specs=vmem,
        scratch_shapes=[
            pltpu.VMEM((slots, block, dip), green.dtype),
            pltpu.VMEM((strike_rows, windows, dip), jnp.bfloat16),
            pltpu.VMEM((slots, windows, block), f32),
            pltpu.VMEM((row_count + 1, windows, block), f32),
            dma((CHUNKS,)),
        ],
        name="forward",
    )(ids, model.reshape(windows * strike_rows, dip), green)

    residual = pl.pallas_call(
        functools.partial(exchange_kernel, n_strike),
        out_shape=jax.ShapeDtypeStruct((sta_rows, samples), f32),
        in_specs=[vmem, vmem],
        out_specs=vmem,
        scratch_shapes=[
            pltpu.VMEM((n_strike, sta_rows, samples), f32),
            dma((n_strike,)),
            dma((n_strike,)),
        ],
        compiler_params=pltpu.CompilerParams(collective_id=0, has_side_effects=True),
        name="exchange",
    )(partial, data)

    grad = pl.pallas_call(
        functools.partial(adjoint_kernel, strike_rows),
        out_shape=jax.ShapeDtypeStruct((windows * strike_rows, dip), f32),
        in_specs=[smem, vmem, hbm],
        out_specs=vmem,
        scratch_shapes=[
            pltpu.VMEM((slots, block, dip), green.dtype),
            pltpu.VMEM((row_count, windows, block), jnp.bfloat16),
            pltpu.VMEM((slots, windows, dip), f32),
            pltpu.VMEM(((strike_rows + 1) * windows, dip), f32),
            dma((CHUNKS,)),
        ],
        name="adjoint",
    )(ids, residual, green)

    depth = n_sta // 4
    own = windows // n_sta
    pieces = min(own, 4)
    parted = (2, 2, depth, own, strike_rows, dip)
    updated = pl.pallas_call(
        functools.partial(reduce_kernel, n_sta, n_strike, pieces),
        out_shape=jax.ShapeDtypeStruct(parted, f32),
        in_specs=[vmem, vmem],
        out_specs=vmem,
        scratch_shapes=[
            pltpu.VMEM((2,) + parted[2:], f32),
            pltpu.VMEM(parted[2:], f32),
            pltpu.VMEM((depth - 1,) + parted[3:], f32),
            pltpu.VMEM((own, strike_rows + 2 * HALO, dip), f32),
            dma((2, pieces)), dma((2, pieces)),
            dma((pieces,)), dma((pieces,)),
            dma((depth - 1, pieces)), dma((depth - 1, pieces)),
            dma((2,)), dma((2,)),
            dma((depth,)), dma((depth,)),
            dma((depth,)), dma((depth,)),
            dma((2, depth)), dma((2, depth)),
        ],
        compiler_params=pltpu.CompilerParams(collective_id=1, has_side_effects=True),
        name="reduce",
    )(grad.reshape(parted), model.reshape(parted))
    return residual, updated.reshape(windows, strike_rows, dip)


def solution(mesh):
    in_specs = (
        P("sta", None),
        P(None, "strike", None),
        P("sta", "strike", None, None, None),
        P("sta", "strike", None),
    )
    out_specs = (P("sta", None), P(None, "strike", None))
    body = functools.partial(local, mesh.shape["sta"], mesh.shape["strike"])
    return jax.shard_map(body, mesh=mesh, in_specs=in_specs, out_specs=out_specs, check_vma=False)
```

time: 230 us -> 56.1 us (0.24)
  waiting for transfers between devices: 99.7 us -> 0 us
  Pallas kernels: 0 us -> 52.1 us
  other arithmetic: 40.9 us -> 0 us
  local copies, waits for them, and re-layouts: 32.3 us -> 2.87 us
  starting transfers between devices: 23.7 us -> 0 us
  between operations: 14.3 us -> 0.68 us
  matrix products: 9.33 us -> 0 us
  blocking collectives: 8.7 us -> 0 us
    psum x1 -> x0, waiting for transfers between devices: 93.6 us -> none  [local(): field = lax.psum(partial_grad, 'sta')]
    pallas_call x0 -> x4, Pallas kernels: none -> 52.1 us  [the longest x1 33.5 us: local(): pl.pallas_call(functools.partial(reduce_kernel, n_sta, n_strike, pieces),...]
    scatter-add x2 -> x0, other arithmetic: 30.1 us -> none  [the longest x1 15.1 us: local(): jax.ops.segment_sum(slot_grads, col_target, num_segments=strike_rows)]
    ppermute x8 -> x0, starting transfers between devices: 23.6 us -> none  [the longest x4 18.4 us: extended(): lax.ppermute(lax.slice_in_dim(block, block.shape[dim] - width, None, axis...]
    reshape x5 -> x0, local copies, waits for them, and re-layouts: 13.8 us -> none  [the longest x1 3.59 us: shear_add(): sheared = flattened.reshape(count_rows, windows, length + windows - 1)]
    dot_general x2 -> x0, matrix products: 9.33 us -> none  [the longest x1 5.28 us: local(): jnp.einsum('cts,wcs->cwt', blocks, columns, preferred_element_type=jnp.fl...]
    psum x1 -> x0, blocking collectives: 8.7 us -> none  [local(): residual = lax.psum(partial_synth, 'strike') - data]
    ppermute x8 -> x0, waiting for transfers between devices: 6.1 us -> none  [the longest x4 6.09 us: extended(): lax.ppermute(lax.slice_in_dim(block, block.shape[dim] - width, None, axis...]
  transfers between devices with their start and end apart: 9 -> 0, of which waited for: 5 -> 0; matrix products, arithmetic and copies ran while one was open for 0% -> 0% of each run, Pallas kernels for 0% -> 0%
where the time goes in v1:
time: 56.1 us; the launch traced here: 55.7 us
  Pallas kernels  52.1 us (93%)
  local copies, waits for them, and re-layouts  2.87 us (5%)
  between operations  0.68 us (1%)
    pallas_call x1, Pallas kernels, local(): pl.pallas_call(functools.partial(reduce_kernel, n_sta, n_strike, pieces),...  33.5 us
    pallas_call x1, Pallas kernels, local(): pl.pallas_call(functools.partial(forward_kernel, strike_rows), out_shape=...  6.72 us
    pallas_call x1, Pallas kernels, local(): pl.pallas_call(functools.partial(exchange_kernel, n_strike), out_shape=ja...  6.07 us
    pallas_call x1, Pallas kernels, local(): pl.pallas_call(functools.partial(adjoint_kernel, strike_rows), out_shape=...  5.8 us
    unnamed x4, local copies, waits for them, and re-layouts  2.87 us

profile of v1, /device:TPU:0, one launch (start us, length us, event | category | flops | bytes accessed | tf_op | source)
XLA Modules:
  0.0 55.7 jit_solution(13172350651011320513)
XLA Ops:
  0.6 6.7 %forward.1.part_ref = f32[8,512]{1,0:T(8,128)} custom-call(s32[96]{0:T(128)} %bitcast.12, f32[2048,128]{1,0:T(8,128)} %bitcast.8, bf16[96,128,128]{2,1,0:T(8,128)(2,1)} %bitcast.6), custom_call_target="tpu_custom_call" | custom-call | tf_op jit(solution)/shard_map/forward/pallas_call | solution.py:283
  7.4 6.1 %exchange.1.resid_ref = f32[8,512]{1,0:T(8,128)} custom-call(f32[8,512]{1,0:T(8,128)} %forward.1.part_ref, f32[8,512]{1,0:T(8,128)} %data_ref.1), custom_call_target="tpu_custom_call" | custom-call | tf_op jit(solution)/shard_map/exchange/pallas_call | solution.py:298
  13.4 0.0 copy-start
  13.5 5.8 %adjoint.1 = f32[2048,128]{1,0:T(8,128)} custom-call(s32[96]{0:T(128)} %bitcast.13, f32[8,512]{1,0:T(8,128)} %exchange.1.resid_ref, bf16[96,128,128]{2,1,0:T(8,128)(2,1)} %bitcast.7), custom_call_target="tpu_custom_call" | custom-call | tf_op jit(solution)/shard_map/adjoint/pallas_call | solution.py:312
  19.3 33.5 %reduce.1 = f32[2,2,4,4,32,128]{5,4,3,2,1,0:T(8,128)} custom-call(f32[2,2,4,4,32,128]{5,4,3,2,1,0:T(8,128)} %bitcast.10, f32[2,2,4,4,32,128]{5,4,3,2,1,0:T(8,128)} %bitcast.9), custom_call_target="tpu_custom_call" | custom-call | tf_op jit(solution)/shard_map/reduce/pallas_call | solution.py:331
  52.8 0.0 copy-done
  52.8 0.6 %copy.8 = f32[8,512]{1,0:T(8,128)} copy(f32[8,512]{1,0:T(8,128)S(1)} %copy-done) | data formatting | bytes 32768
  53.4 2.3 %copy.9 = f32[64,32,128]{2,1,0:T(8,128)} copy(f32[64,32,128]{2,1,0:T(8,128)} %bitcast.11) | data formatting | bytes 2097152
Async XLA Ops:
  13.4 39.4 %copy-start = (f32[8,512]{1,0:T(8,128)S(1)}, f32[8,512]{1,0:T(8,128)}, u32[]{:S(2)}) copy-start(f32[8,512]{1,0:T(8,128)} %exchange.1.resid_ref) | copy-start | bytes 49156

commit v2 on v1

--- a/solution.py
+++ b/solution.py
@@ -13,6 +13,7 @@
 MESH = pl.DeviceIdType.MESH
 CHUNKS = 6
 HALO = 8
+VMEM_LIMIT = 16 * 2**20
 
 
 def green_copy(green_ref, gbuf, sems, i, size):
@@ -21,16 +22,19 @@
     )
 
 
-def forward_kernel(strike_rows, ids_ref, model_ref, green_ref, out_ref, gbuf, cols, prod, acc, sems):
+def forward_kernel(strike_rows, ids_ref, model_hbm, green_ref, out_ref, model_ref, gbuf, cols, prod, acc, model_sem, sems):
     slots, block = gbuf.shape[:2]
     windows = cols.shape[1]
     sta_rows, samples = out_ref.shape
     time_blocks = samples // block
     row_count = sta_rows * time_blocks
     size = slots // CHUNKS
+    model_copy = pltpu.make_async_copy(model_hbm, model_ref, model_sem)
+    model_copy.start()
     for i in range(CHUNKS):
         green_copy(green_ref, gbuf, sems, i, size).start()
     acc[...] = jnp.zeros_like(acc)
+    model_copy.wait()
     for q in range(strike_rows):
         cols[q] = model_ref[pl.ds(q, windows, stride=strike_rows), :].astype(jnp.bfloat16)
 
@@ -64,14 +68,12 @@
             before = rolled
 
 
-def adjoint_kernel(strike_rows, ids_ref, resid_ref, green_ref, out_ref, gbuf, rows, prod, acc, sems):
-    slots, block = gbuf.shape[:2]
+def adjoint_kernel(strike_rows, ids_ref, resid_ref, green_ref, out_ref, rows, prod, acc):
+    slots, block = green_ref.shape[:2]
     windows = rows.shape[1]
     sta_rows, samples = resid_ref.shape
     time_blocks = samples // block
     size = slots // CHUNKS
-    for i in range(CHUNKS):
-        green_copy(green_ref, gbuf, sems, i, size).start()
     acc[...] = jnp.zeros_like(acc)
     back = windows - 1 - lax.broadcasted_iota(jnp.int32, (windows, block), 0)
     same = lax.broadcasted_iota(jnp.int32, (windows, block), 1) + back < block
@@ -85,11 +87,10 @@
 
     @pl.loop(0, CHUNKS)
     def _(i):
-        green_copy(green_ref, gbuf, sems, i, size).wait()
         for u in range(size):
             c = i * size + u
             row = lax.div(jnp.maximum(ids_ref[c], 0), strike_rows)
-            prod[c] = jnp.dot(rows[row], gbuf[c], preferred_element_type=jnp.float32)
+            prod[c] = jnp.dot(rows[row], green_ref[c], preferred_element_type=jnp.float32)
 
     @pl.loop(0, slots, step=4)
     def _(base):
@@ -135,7 +136,7 @@
 
 
 def reduce_kernel(
-    n_sta, n_strike, pieces, grad_ref, model_ref, out_ref, from_core, from_x, from_z, ext,
+    n_sta, n_strike, pieces, grad_ref, out_ref, from_core, from_x, from_z, ext,
     core_s, core_r, x_s, x_r, z_s, z_r, halo_s, halo_r, gz_s, gz_r, gx_s, gx_r, gc_s, gc_r,
 ):
     depth = n_sta // 4
@@ -231,36 +232,62 @@
         halo_r.at[1],
         down_dev,
     )
-    tall = rows + 2 * HALO
-    row = lax.broadcasted_iota(jnp.int32, (own, tall, dip), 1)
-    lane = lax.broadcasted_iota(jnp.int32, (own, tall, dip), 2)
-    first = jnp.where(strike > 0, 0, HALO)
-    last = jnp.where(strike < n_strike - 1, tall, HALO + rows)
-    inside = (row >= first) & (row < last)
+
+    def diffuse(v, inside):
+        tall = v.shape[1]
+        lane = lax.broadcasted_iota(jnp.int32, v.shape, 2)
+        for _ in range(SWEEPS):
+            left = jnp.where(lane > 0, pltpu.roll(v, 1, 2), 0.0)
+            right = jnp.where(lane < dip - 1, pltpu.roll(v, dip - 1, 2), 0.0)
+            around = pltpu.roll(v, tall - 1, 1) + pltpu.roll(v, 1, 1) + right + left - 4.0 * v
+            v = v + NU_DIFF * around
+            if inside is not None:
+                v = jnp.where(inside, v, 0.0)
+        return v
+
+    mid = diffuse(field, None)
+    out_ref[core, x, z, :, HALO : rows - HALO] = STEP_LEN * mid[:, HALO : rows - HALO]
+
+    spans = ((HALO, rows - 2 * HALO), (0, HALO), (rows - HALO, HALO))
+
+    def view(a, b, c, j):
+        return out_ref.at[a, b, c, :, pl.ds(*spans[j])]
+
+    fetched, crossed, to_core = {}, {}, []
+
+    def give(j, d):
+        block = view(core, x, lax.rem(z - d + depth, depth), j)
+        crossed[j, d] = send(block, block, gx_s.at[j, d], gx_r.at[j, d], x_dev)
+        to_core.append(send(block, block, gc_s.at[0, j, d], gc_r.at[0, j, d], core_dev))
+
+    def spread(j):
+        block = view(core, x, z, j)
+        for d in range(1, depth):
+            fetched[j, d] = send(block, block, gz_s.at[j, d], gz_r.at[j, d], z_dev(d))
+        give(j, 0)
+
+    spread(0)
     high.wait_recv()
     low.wait_recv()
-    v = jnp.where(inside, ext[...], 0.0)
-    for _ in range(SWEEPS):
-        left = jnp.where(lane > 0, pltpu.roll(v, 1, 2), 0.0)
-        right = jnp.where(lane < dip - 1, pltpu.roll(v, dip - 1, 2), 0.0)
-        around = pltpu.roll(v, tall - 1, 1) + pltpu.roll(v, 1, 1) + right + left - 4.0 * v
-        v = jnp.where(inside, v + NU_DIFF * around, 0.0)
-    out_ref[core, x, z] = model_ref[core, x, z] - STEP_LEN * v[:, HALO : HALO + rows]
-
-    mine = out_ref.at[core, x, z]
-    fetched = [send(mine, mine, gz_s.at[d], gz_r.at[d], z_dev(d)) for d in range(1, depth)]
-    crossed = []
-    to_core = []
-    for d in range(depth):
-        if d:
-            fetched[d - 1].wait_recv()
-        block = out_ref.at[core, x, lax.rem(z - d + depth, depth)]
-        crossed.append(send(block, block, gx_s.at[d], gx_r.at[d], x_dev))
-        to_core.append(send(block, block, gc_s.at[0, d], gc_r.at[0, d], core_dev))
-    for d in range(depth):
-        crossed[d].wait_recv()
-        block = out_ref.at[core, other_x, lax.rem(z - d + depth, depth)]
-        to_core.append(send(block, block, gc_s.at[1, d], gc_r.at[1, d], core_dev))
+    for j, start in ((1, 0), (2, rows - HALO)):
+        strip = ext[:, start : start + 3 * HALO]
+        row = lax.broadcasted_iota(jnp.int32, strip.shape, 1)
+        if j == 1:
+            inside = row >= jnp.where(strike > 0, 0, HALO)
+        else:
+            inside = row < jnp.where(strike < n_strike - 1, 3 * HALO, 2 * HALO)
+        strip = diffuse(jnp.where(inside, strip, 0.0), inside)
+        out_ref[core, x, z, :, spans[j][0] : spans[j][0] + HALO] = STEP_LEN * strip[:, HALO : 2 * HALO]
+        spread(j)
+    for j in range(3):
+        for d in range(1, depth):
+            fetched[j, d].wait_recv()
+            give(j, d)
+    for j in range(3):
+        for d in range(depth):
+            crossed[j, d].wait_recv()
+            block = view(core, other_x, lax.rem(z - d + depth, depth), j)
+            to_core.append(send(block, block, gc_s.at[1, j, d], gc_r.at[1, j, d], core_dev))
     for copy in to_core:
         copy.wait_recv()
     for copy in started:
@@ -283,13 +310,15 @@
     partial = pl.pallas_call(
         functools.partial(forward_kernel, strike_rows),
         out_shape=jax.ShapeDtypeStruct((sta_rows, samples), f32),
-        in_specs=[smem, vmem, hbm],
+        in_specs=[smem, hbm, hbm],
         out_specs=vmem,
         scratch_shapes=[
+            pltpu.VMEM((windows * strike_rows, dip), f32),
             pltpu.VMEM((slots, block, dip), green.dtype),
             pltpu.VMEM((strike_rows, windows, dip), jnp.bfloat16),
             pltpu.VMEM((slots, windows, block), f32),
             pltpu.VMEM((row_count + 1, windows, block), f32),
+            dma,
             dma((CHUNKS,)),
         ],
         name="forward",
@@ -305,22 +334,21 @@
             dma((n_strike,)),
             dma((n_strike,)),
         ],
-        compiler_params=pltpu.CompilerParams(collective_id=0, has_side_effects=True),
+        compiler_params=pltpu.CompilerParams(collective_id=0, has_side_effects=True, vmem_limit_bytes=VMEM_LIMIT),
         name="exchange",
     )(partial, data)
 
     grad = pl.pallas_call(
         functools.partial(adjoint_kernel, strike_rows),
         out_shape=jax.ShapeDtypeStruct((windows * strike_rows, dip), f32),
-        in_specs=[smem, vmem, hbm],
+        in_specs=[smem, vmem, vmem],
         out_specs=vmem,
         scratch_shapes=[
-            pltpu.VMEM((slots, block, dip), green.dtype),
             pltpu.VMEM((row_count, windows, block), jnp.bfloat16),
             pltpu.VMEM((slots, windows, dip), f32),
             pltpu.VMEM(((strike_rows + 1) * windows, dip), f32),
-            dma((CHUNKS,)),
         ],
+        compiler_params=pltpu.CompilerParams(vmem_limit_bytes=VMEM_LIMIT),
         name="adjoint",
     )(ids, residual, green)
 
@@ -328,10 +356,10 @@
     own = windows // n_sta
     pieces = min(own, 4)
     parted = (2, 2, depth, own, strike_rows, dip)
-    updated = pl.pallas_call(
+    field = pl.pallas_call(
         functools.partial(reduce_kernel, n_sta, n_strike, pieces),
         out_shape=jax.ShapeDtypeStruct(parted, f32),
-        in_specs=[vmem, vmem],
+        in_specs=[vmem],
         out_specs=vmem,
         scratch_shapes=[
             pltpu.VMEM((2,) + parted[2:], f32),
@@ -342,14 +370,15 @@
             dma((pieces,)), dma((pieces,)),
             dma((depth - 1, pieces)), dma((depth - 1, pieces)),
             dma((2,)), dma((2,)),
-            dma((depth,)), dma((depth,)),
-            dma((depth,)), dma((depth,)),
-            dma((2, depth)), dma((2, depth)),
+            dma((3, depth)), dma((3, depth)),
+            dma((3, depth)), dma((3, depth)),
+            dma((2, 3, depth)), dma((2, 3, depth)),
         ],
-        compiler_params=pltpu.CompilerParams(collective_id=1, has_side_effects=True),
+        compiler_params=pltpu.CompilerParams(collective_id=1, has_side_effects=True, vmem_limit_bytes=VMEM_LIMIT),
         name="reduce",
-    )(grad.reshape(parted), model.reshape(parted))
-    return residual, updated.reshape(windows, strike_rows, dip)
+    )(grad.reshape(parted))
+    updated = model - field.reshape(windows, strike_rows, dip)
+    return residual, updated
 
 
 def solution(mesh):

time: 56.1 us -> 49.2 us (0.88)
  Pallas kernels: 52.1 us -> 45.7 us
  local copies, waits for them, and re-layouts: 2.87 us -> 1.34 us
  other arithmetic: 0 us -> 1.19 us
    pallas_call x1, Pallas kernels: 33.5 us -> 29.2 us  [local(): pl.pallas_call(functools.partial(reduce_kernel, n_sta, n_strike, pieces),...]
    pallas_call x1, Pallas kernels: 5.8 us -> 3.69 us  [local(): pl.pallas_call(functools.partial(adjoint_kernel, strike_rows), out_shape=...]
    unnamed x4 -> x11, local copies, waits for them, and re-layouts: 2.87 us -> 1.34 us
    pallas_call x1, Pallas kernels: 6.07 us -> 4.76 us  [local(): pl.pallas_call(functools.partial(exchange_kernel, n_strike), out_shape=ja...]
    pallas_call x1, Pallas kernels: 6.72 us -> 7.98 us  [local(): pl.pallas_call(functools.partial(forward_kernel, strike_rows), out_shape=...]
    sub x0 -> x1, other arithmetic: none -> 1.19 us  [local(): updated = model - field.reshape(windows, strike_rows, dip)]
where the time goes in v2:
time: 49.2 us; the launch traced here: 48.9 us
  Pallas kernels  45.7 us (93%)
  local copies, waits for them, and re-layouts  1.34 us (3%)
  other arithmetic  1.19 us (2%)
  between operations  0.73 us (1%)
    pallas_call x1, Pallas kernels, local(): pl.pallas_call(functools.partial(reduce_kernel, n_sta, n_strike, pieces),...  29.2 us
    pallas_call x1, Pallas kernels, local(): pl.pallas_call(functools.partial(forward_kernel, strike_rows), out_shape=...  7.98 us
    pallas_call x1, Pallas kernels, local(): pl.pallas_call(functools.partial(exchange_kernel, n_strike), out_shape=ja...  4.76 us
    pallas_call x1, Pallas kernels, local(): pl.pallas_call(functools.partial(adjoint_kernel, strike_rows), out_shape=...  3.69 us
    unnamed x11, local copies, waits for them, and re-layouts  1.34 us
    sub x1, other arithmetic, local(): updated = model - field.reshape(windows, strike_rows, dip)  1.19 us

profile of v2, /device:TPU:0, one launch (start us, length us, event | category | flops | bytes accessed | tf_op | source)
XLA Modules:
  0.0 48.9 jit_solution(10724530922653492363)
XLA Ops:
  0.6 0.0 copy-start.3
  0.6 0.0 copy-start
  0.6 0.0 copy-start.2
  0.7 8.0 %forward.1.part_ref = f32[8,512]{1,0:T(8,128)} custom-call(s32[96]{0:T(128)} %bitcast.9, f32[2048,128]{1,0:T(8,128)} %bitcast.11, bf16[96,128,128]{2,1,0:T(8,128)(2,1)} %bitcast.6), custom_call_target="tpu_custom_call" | custom-call | tf_op jit(solution)/shard_map/forward/pallas_call | solution.py:310
  8.6 0.0 copy-done.2
  8.7 0.0 copy-start.1
  8.7 0.7 %copy-done.1 = f32[8,512]{1,0:T(8,128)S(1)} copy-done((f32[8,512]{1,0:T(8,128)S(1)}, f32[8,512]{1,0:T(8,128)}, u32[]{:S(2)}) %copy-start.1) | copy-done | bytes 16408
  9.4 4.8 %exchange.1.resid_ref = f32[8,512]{1,0:T(8,128)S(1)} custom-call(f32[8,512]{1,0:T(8,128)S(1)} %copy-done.1, f32[8,512]{1,0:T(8,128)S(1)} %copy-done.2), custom_call_target="tpu_custom_call" | custom-call | tf_op jit(solution)/shard_map/exchange/pallas_call | solution.py:327
  14.1 0.0 copy-done.3
  14.2 0.0 copy-done
  14.2 0.0 copy-start.4
  14.2 3.7 %adjoint.1 = f32[2048,128]{1,0:T(8,128)S(1)} custom-call(s32[96]{0:T(128)S(1)} %bitcast.10, f32[8,512]{1,0:T(8,128)S(1)} %exchange.1.resid_ref, bf16[96,128,128]{2,1,0:T(8,128)(2,1)S(1)} %bitcast.7), custom_call_target="tpu_custom_call" | custom-call | tf_op jit(solution)/shard_map/adjoint/pallas_call | solution.py:341
  17.9 29.2 %reduce.1 = f32[2,2,4,4,32,128]{5,4,3,2,1,0:T(8,128)S(1)} custom-call(f32[2,2,4,4,32,128]{5,4,3,2,1,0:T(8,128)S(1)} %bitcast.8), custom_call_target="tpu_custom_call" | custom-call | tf_op jit(solution)/shard_map/reduce/pallas_call | solution.py:359
  47.1 0.0 copy-done.4
  47.1 1.2 %bitcast_subtract_fusion = f32[64,32,128]{2,1,0:T(8,128)} fusion(f32[64,32,128]{2,1,0:T(8,128)S(1)} %copy-done.4, f32[2,2,4,4,32,128]{5,4,3,2,1,0:T(8,128)S(1)} %reduce.1), kind=kLoop, calls=%fused_computation | loop fusion | flops 262144 | bytes 3145728 | tf_op jit(solution)/shard_map/sub | solution.py:380
  48.3 0.6 %copy.7 = f32[8,512]{1,0:T(8,128)} copy(f32[8,512]{1,0:T(8,128)S(1)} %exchange.1.resid_ref) | data formatting | bytes 32768
Async XLA Ops:
  0.6 13.5 %copy-start.3 = (s32[1,1,96]{2,1,0:T(1,128)S(1)}, s32[1,1,96]{2,1,0:T(1,128)}, u32[]{:S(2)}) copy-start(s32[1,1,96]{2,1,0:T(1,128)} %param.7) | copy-start | bytes 1156
  0.6 13.5 %copy-start = (bf16[1,1,96,128,128]{4,3,2,1,0:T(8,128)(2,1)S(1)}, bf16[1,1,96,128,128]{4,3,2,1,0:T(8,128)(2,1)}, u32[]{:S(2)}) copy-start(bf16[1,1,96,128,128]{4,3,2,1,0:T(8,128)(2,1)} %param.6) | copy-start | bytes 9437188
  0.6 8.0 %copy-start.2 = (f32[8,512]{1,0:T(8,128)S(1)}, f32[8,512]{1,0:T(8,128)}, u32[]{:S(2)}) copy-start(f32[8,512]{1,0:T(8,128)} %data_ref.1) | copy-start | bytes 49156
  8.7 0.7 %copy-start.1 = (f32[8,512]{1,0:T(8,128)S(1)}, f32[8,512]{1,0:T(8,128)}, u32[]{:S(2)}) copy-start(f32[8,512]{1,0:T(8,128)} %forward.1.part_ref) | copy-start | bytes 49156
  14.2 33.0 %copy-start.4 = (f32[64,32,128]{2,1,0:T(8,128)S(1)}, f32[64,32,128]{2,1,0:T(8,128)}, u32[]{:S(2)}) copy-start(f32[64,32,128]{2,1,0:T(8,128)} %param.5) | copy-start | bytes 3145732

commit v3 on v2

--- a/solution.py
+++ b/solution.py
@@ -22,7 +22,7 @@
     )
 
 
-def forward_kernel(strike_rows, ids_ref, model_hbm, green_ref, out_ref, model_ref, gbuf, cols, prod, acc, model_sem, sems):
+def forward_kernel(strike_rows, ids_ref, model_hbm, green_ref, out_ref, gbuf, model_ref, cols, prod, acc, model_sem, sems):
     slots, block = gbuf.shape[:2]
     windows = cols.shape[1]
     sta_rows, samples = out_ref.shape
@@ -68,12 +68,13 @@
             before = rolled
 
 
-def adjoint_kernel(strike_rows, ids_ref, resid_ref, green_ref, out_ref, rows, prod, acc):
+def adjoint_kernel(strike_rows, ids_ref, synth_ref, data_ref, green_ref, resid_ref, acc, rows, prod):
     slots, block = green_ref.shape[:2]
     windows = rows.shape[1]
     sta_rows, samples = resid_ref.shape
     time_blocks = samples // block
     size = slots // CHUNKS
+    resid_ref[...] = synth_ref[...] - data_ref[...]
     acc[...] = jnp.zeros_like(acc)
     back = windows - 1 - lax.broadcasted_iota(jnp.int32, (windows, block), 0)
     same = lax.broadcasted_iota(jnp.int32, (windows, block), 1) + back < block
@@ -100,13 +101,8 @@
             here = pl.ds(pl.multiple_of(q * windows, windows), windows)
             acc[here, :] = acc[here, :] + prod[base + u]
 
-    for w in range(windows):
-        out_ref[w * strike_rows : (w + 1) * strike_rows, :] = acc[
-            pl.ds(windows - 1 - w, strike_rows, stride=windows), :
-        ]
-
-
-def exchange_kernel(n, part_ref, data_ref, out_ref, parts, send, recv):
+
+def exchange_kernel(n, part_ref, out_ref, parts, send, recv):
     me = lax.axis_index("strike")
     barrier = pltpu.get_barrier_semaphore()
     for d in range(1, n):
@@ -132,17 +128,19 @@
     total = parts[lax.rem(me, n)]
     for j in range(1, n):
         total = total + parts[lax.rem(me - j + n, n)]
-    out_ref[...] = total - data_ref[...]
+    out_ref[...] = total
 
 
 def reduce_kernel(
-    n_sta, n_strike, pieces, grad_ref, out_ref, from_core, from_x, from_z, ext,
+    n_sta, n_strike, acc_ref, out_ref, grad_ref, from_core, from_x, from_z, ext,
     core_s, core_r, x_s, x_r, z_s, z_r, halo_s, halo_r, gz_s, gz_r, gx_s, gx_r, gc_s, gc_r,
 ):
     depth = n_sta // 4
     own = grad_ref.shape[3]
+    halves_of_rows = 2
+    pieces = own * halves_of_rows
     rows, dip = grad_ref.shape[4:]
-    part = own // pieces
+    part = rows // halves_of_rows
     sta = lax.axis_index("sta")
     strike = lax.axis_index("strike")
     core = lax.rem(sta, 2)
@@ -164,6 +162,10 @@
     barrier = pltpu.get_barrier_semaphore()
     for peer in peers:
         pl.semaphore_signal(barrier, inc=1, device_id=peer, device_id_type=MESH)
+    windows = 4 * depth * own
+    for w in range(windows):
+        place = (w // (windows // 2), w // (windows // 4) % 2, w // own % depth, w % own)
+        grad_ref[place] = acc_ref[pl.ds(windows - 1 - w, rows, stride=windows), :]
     pl.semaphore_wait(barrier, len(peers))
 
     started = []
@@ -177,15 +179,15 @@
         return copy
 
     def cut(k):
-        return pl.ds(k * part, part)
+        return (pl.ds(k // halves_of_rows, 1), pl.ds(k % halves_of_rows * part, part))
 
     halves = []
     for h, side in enumerate((other_x, x)):
         for k in range(pieces):
             halves.append(
                 send(
-                    grad_ref.at[other_core, side, :, cut(k)],
-                    from_core.at[h, :, cut(k)],
+                    grad_ref.at[other_core, side, :, *cut(k)],
+                    from_core.at[h, :, *cut(k)],
                     core_s.at[h, k],
                     core_r.at[h, k],
                     core_dev,
@@ -194,22 +196,22 @@
     across = []
     for k in range(pieces):
         halves[k].wait_recv()
-        from_core[0, :, cut(k)] = from_core[0, :, cut(k)] + grad_ref[core, other_x, :, cut(k)]
+        from_core[0, :, *cut(k)] = from_core[0, :, *cut(k)] + grad_ref[core, other_x, :, *cut(k)]
         across.append(
-            send(from_core.at[0, :, cut(k)], from_x.at[:, cut(k)], x_s.at[k], x_r.at[k], x_dev)
+            send(from_core.at[0, :, *cut(k)], from_x.at[:, *cut(k)], x_s.at[k], x_r.at[k], x_dev)
         )
     for k in range(pieces):
         halves[pieces + k].wait_recv()
-        from_core[1, :, cut(k)] = from_core[1, :, cut(k)] + grad_ref[core, x, :, cut(k)]
+        from_core[1, :, *cut(k)] = from_core[1, :, *cut(k)] + grad_ref[core, x, :, *cut(k)]
     along = []
     for k in range(pieces):
         across[k].wait_recv()
-        from_x[:, cut(k)] = from_x[:, cut(k)] + from_core[1, :, cut(k)]
+        from_x[:, *cut(k)] = from_x[:, *cut(k)] + from_core[1, :, *cut(k)]
         for d in range(1, depth):
             along.append(
                 send(
-                    from_x.at[z_at(d), cut(k)],
-                    from_z.at[d - 1, cut(k)],
+                    from_x.at[z_at(d), *cut(k)],
+                    from_z.at[d - 1, *cut(k)],
                     z_s.at[d - 1, k],
                     z_r.at[d - 1, k],
                     z_dev(d),
@@ -307,27 +309,34 @@
     f32 = jnp.float32
     dma = pltpu.SemaphoreType.DMA
 
-    partial = pl.pallas_call(
+    partial, green = pl.pallas_call(
         functools.partial(forward_kernel, strike_rows),
-        out_shape=jax.ShapeDtypeStruct((sta_rows, samples), f32),
+        out_shape=(
+            jax.ShapeDtypeStruct((sta_rows, samples), f32),
+            jax.ShapeDtypeStruct((slots, block, dip), green.dtype),
+        ),
         in_specs=[smem, hbm, hbm],
-        out_specs=vmem,
+        out_specs=(vmem, vmem),
         scratch_shapes=[
             pltpu.VMEM((windows * strike_rows, dip), f32),
-            pltpu.VMEM((slots, block, dip), green.dtype),
             pltpu.VMEM((strike_rows, windows, dip), jnp.bfloat16),
             pltpu.VMEM((slots, windows, block), f32),
             pltpu.VMEM((row_count + 1, windows, block), f32),
             dma,
             dma((CHUNKS,)),
         ],
+        compiler_params=pltpu.CompilerParams(vmem_limit_bytes=VMEM_LIMIT),
         name="forward",
-    )(ids, model.reshape(windows * strike_rows, dip), green)
-
-    residual = pl.pallas_call(
+    )(
+        ids,
+        pltpu.with_memory_space_constraint(model.reshape(windows * strike_rows, dip), pltpu.HBM),
+        pltpu.with_memory_space_constraint(green, pltpu.HBM),
+    )
+
+    synthetic = pl.pallas_call(
         functools.partial(exchange_kernel, n_strike),
         out_shape=jax.ShapeDtypeStruct((sta_rows, samples), f32),
-        in_specs=[vmem, vmem],
+        in_specs=[vmem],
         out_specs=vmem,
         scratch_shapes=[
             pltpu.VMEM((n_strike, sta_rows, samples), f32),
@@ -336,32 +345,35 @@
         ],
         compiler_params=pltpu.CompilerParams(collective_id=0, has_side_effects=True, vmem_limit_bytes=VMEM_LIMIT),
         name="exchange",
-    )(partial, data)
-
-    grad = pl.pallas_call(
+    )(partial)
+
+    residual, grad = pl.pallas_call(
         functools.partial(adjoint_kernel, strike_rows),
-        out_shape=jax.ShapeDtypeStruct((windows * strike_rows, dip), f32),
-        in_specs=[smem, vmem, vmem],
-        out_specs=vmem,
+        out_shape=(
+            jax.ShapeDtypeStruct((sta_rows, samples), f32),
+            jax.ShapeDtypeStruct(((strike_rows + 1) * windows, dip), f32),
+        ),
+        in_specs=[smem, vmem, vmem, vmem],
+        out_specs=(vmem, vmem),
         scratch_shapes=[
             pltpu.VMEM((row_count, windows, block), jnp.bfloat16),
             pltpu.VMEM((slots, windows, dip), f32),
-            pltpu.VMEM(((strike_rows + 1) * windows, dip), f32),
         ],
         compiler_params=pltpu.CompilerParams(vmem_limit_bytes=VMEM_LIMIT),
         name="adjoint",
-    )(ids, residual, green)
+    )(ids, synthetic, data, green)
 
     depth = n_sta // 4
     own = windows // n_sta
-    pieces = min(own, 4)
+    pieces = 2 * own
     parted = (2, 2, depth, own, strike_rows, dip)
     field = pl.pallas_call(
-        functools.partial(reduce_kernel, n_sta, n_strike, pieces),
+        functools.partial(reduce_kernel, n_sta, n_strike),
         out_shape=jax.ShapeDtypeStruct(parted, f32),
         in_specs=[vmem],
         out_specs=vmem,
         scratch_shapes=[
+            pltpu.VMEM(parted, f32),
             pltpu.VMEM((2,) + parted[2:], f32),
             pltpu.VMEM(parted[2:], f32),
             pltpu.VMEM((depth - 1,) + parted[3:], f32),
@@ -376,7 +388,7 @@
         ],
         compiler_params=pltpu.CompilerParams(collective_id=1, has_side_effects=True, vmem_limit_bytes=VMEM_LIMIT),
         name="reduce",
-    )(grad.reshape(parted))
+    )(grad)
     updated = model - field.reshape(windows, strike_rows, dip)
     return residual, updated
 

time: 49.2 us -> 47.5 us (0.965)
  Pallas kernels: 45.7 us -> 44.7 us
  local copies, waits for them, and re-layouts: 1.34 us -> 0.66 us
    pallas_call x1, Pallas kernels: 7.98 us -> 7 us  [local(): pl.pallas_call(functools.partial(forward_kernel, strike_rows), out_shape=...]
    unnamed x11 -> x6, local copies, waits for them, and re-layouts: 1.34 us -> 0.66 us
where the time goes in v3:
time: 47.5 us; the launch traced here: 47.3 us
  Pallas kernels  44.7 us (94%)
  other arithmetic  1.19 us (3%)
  between operations  0.69 us (1%)
  local copies, waits for them, and re-layouts  0.66 us (1%)
    pallas_call x1, Pallas kernels, local(): pl.pallas_call(functools.partial(reduce_kernel, n_sta, n_strike), out_sha...  29.2 us
    pallas_call x1, Pallas kernels, local(): pl.pallas_call(functools.partial(forward_kernel, strike_rows), out_shape=...  7 us
    pallas_call x1, Pallas kernels, local(): pl.pallas_call(functools.partial(exchange_kernel, n_strike), out_shape=ja...  4.81 us
    pallas_call x1, Pallas kernels, local(): pl.pallas_call(functools.partial(adjoint_kernel, strike_rows), out_shape=...  3.7 us
    sub x1, other arithmetic, local(): updated = model - field.reshape(windows, strike_rows, dip)  1.19 us

profile of v3, /device:TPU:0, one launch (start us, length us, event | category | flops | bytes accessed | tf_op | source)
XLA Modules:
  0.0 47.3 jit_solution(1826576334575767609)
XLA Ops:
  0.6 0.0 copy-start
  0.6 0.0 copy-start.1
  0.6 0.7 %copy-done.1 = s32[1,1,96]{2,1,0:T(1,128)S(1)} copy-done((s32[1,1,96]{2,1,0:T(1,128)S(1)}, s32[1,1,96]{2,1,0:T(1,128)}, u32[]{:S(2)}) %copy-start.1) | copy-done | bytes 408
  1.3 7.0 %forward.1 = (f32[8,512]{1,0:T(8,128)S(1)}, bf16[96,128,128]{2,1,0:T(8,128)(2,1)S(1)}) custom-call(s32[96]{0:T(128)S(1)} %bitcast.5, f32[2048,128]{1,0:T(8,128)} %bitcast.7, bf16[96,128,128]{2,1,0:T(8,128)(2,1)} %bitcast.8), custom_call_target="tpu_custom_call" | custom-call | tf_op jit(solution)/shard_map/forward/pallas_call | solution.py:312
  8.3 0.0 copy-start.2
  8.3 4.8 %exchange.1.synth_ref = f32[8,512]{1,0:T(8,128)S(1)} custom-call(f32[8,512]{1,0:T(8,128)S(1)} %get-tuple-element.6.part_ref), custom_call_target="tpu_custom_call" | custom-call | tf_op jit(solution)/shard_map/exchange/pallas_call | solution.py:336
  13.1 0.0 copy-done
  13.2 3.7 %adjoint.1 = (f32[8,512]{1,0:T(8,128)}, f32[2112,128]{1,0:T(8,128)S(1)}) custom-call(s32[96]{0:T(128)S(1)} %bitcast.6, f32[8,512]{1,0:T(8,128)S(1)} %exchange.1.synth_ref, f32[8,512]{1,0:T(8,128)S(1)} %copy-done, bf16[96,128,128]{2,1,0:T(8,128)(2,1)S(1)} %get-tuple-element.7.green_ref), custom_call_target="tpu_custom_call" | custom-call | tf_op jit(solution)/shard_map/adjoint/pallas_call | solution.py:350
  16.9 29.2 %reduce.1 = f32[2,2,4,4,32,128]{5,4,3,2,1,0:T(8,128)S(1)} custom-call(f32[2112,128]{1,0:T(8,128)S(1)} %get-tuple-element.9.acc_ref), custom_call_target="tpu_custom_call" | custom-call | tf_op jit(solution)/shard_map/reduce/pallas_call | solution.py:370
  46.1 0.0 copy-done.2
  46.1 1.2 %bitcast_subtract_fusion = f32[64,32,128]{2,1,0:T(8,128)} fusion(f32[64,32,128]{2,1,0:T(8,128)S(1)} %copy-done.2, f32[2,2,4,4,32,128]{5,4,3,2,1,0:T(8,128)S(1)} %reduce.1), kind=kLoop, calls=%fused_computation | loop fusion | flops 262144 | bytes 3145728 | tf_op jit(solution)/shard_map/sub | solution.py:392
Async XLA Ops:
  0.6 12.5 %copy-start = (f32[8,512]{1,0:T(8,128)S(1)}, f32[8,512]{1,0:T(8,128)}, u32[]{:S(2)}) copy-start(f32[8,512]{1,0:T(8,128)} %data_ref.1) | copy-start | bytes 49156
  0.6 0.7 %copy-start.1 = (s32[1,1,96]{2,1,0:T(1,128)S(1)}, s32[1,1,96]{2,1,0:T(1,128)}, u32[]{:S(2)}) copy-start(s32[1,1,96]{2,1,0:T(1,128)} %param.7) | copy-start | bytes 1156
  8.3 37.8 %copy-start.2 = (f32[64,32,128]{2,1,0:T(8,128)S(1)}, f32[64,32,128]{2,1,0:T(8,128)}, u32[]{:S(2)}) copy-start(f32[64,32,128]{2,1,0:T(8,128)} %param.5) | copy-start | bytes 3145732

commit v4 on v3

--- a/solution.py
+++ b/solution.py
@@ -22,7 +22,7 @@
     )
 
 
-def forward_kernel(strike_rows, ids_ref, model_hbm, green_ref, out_ref, gbuf, model_ref, cols, prod, acc, model_sem, sems):
+def forward_kernel(strike_rows, ids_ref, model_hbm, green_ref, out_ref, gbuf, model_ref, cols, acc, model_sem, sems):
     slots, block = gbuf.shape[:2]
     windows = cols.shape[1]
     sta_rows, samples = out_ref.shape
@@ -43,17 +43,16 @@
         green_copy(green_ref, gbuf, sems, i, size).wait()
         for u in range(size):
             c = i * size + u
-            q = lax.rem(jnp.maximum(ids_ref[c], 0), strike_rows)
-            prod[c] = lax.dot_general(
-                cols[q], gbuf[c], (((1,), (1,)), ((), ())), preferred_element_type=jnp.float32
+            slot_id = ids_ref[c]
+            safe = jnp.maximum(slot_id, 0)
+            term = lax.dot_general(
+                cols[lax.rem(safe, strike_rows)],
+                gbuf[c],
+                (((1,), (1,)), ((), ())),
+                preferred_element_type=jnp.float32,
             )
-
-    @pl.loop(0, slots, step=4)
-    def _(base):
-        for u in range(4):
-            slot_id = ids_ref[base + u]
-            row = jnp.where(slot_id >= 0, lax.div(jnp.maximum(slot_id, 0), strike_rows), row_count)
-            acc[row] = acc[row] + prod[base + u]
+            row = jnp.where(slot_id >= 0, lax.div(safe, strike_rows), row_count)
+            acc[row] = acc[row] + term
 
     window = lax.broadcasted_iota(jnp.int32, (windows, block), 0)
     lane = lax.broadcasted_iota(jnp.int32, (windows, block), 1)
@@ -68,7 +67,7 @@
             before = rolled
 
 
-def adjoint_kernel(strike_rows, ids_ref, synth_ref, data_ref, green_ref, resid_ref, acc, rows, prod):
+def adjoint_kernel(strike_rows, ids_ref, synth_ref, data_ref, green_ref, resid_ref, acc, rows):
     slots, block = green_ref.shape[:2]
     windows = rows.shape[1]
     sta_rows, samples = resid_ref.shape
@@ -90,16 +89,14 @@
     def _(i):
         for u in range(size):
             c = i * size + u
-            row = lax.div(jnp.maximum(ids_ref[c], 0), strike_rows)
-            prod[c] = jnp.dot(rows[row], green_ref[c], preferred_element_type=jnp.float32)
-
-    @pl.loop(0, slots, step=4)
-    def _(base):
-        for u in range(4):
-            slot_id = ids_ref[base + u]
-            q = jnp.where(slot_id >= 0, lax.rem(jnp.maximum(slot_id, 0), strike_rows), strike_rows)
+            slot_id = ids_ref[c]
+            safe = jnp.maximum(slot_id, 0)
+            term = jnp.dot(
+                rows[lax.div(safe, strike_rows)], green_ref[c], preferred_element_type=jnp.float32
+            )
+            q = jnp.where(slot_id >= 0, lax.rem(safe, strike_rows), strike_rows)
             here = pl.ds(pl.multiple_of(q * windows, windows), windows)
-            acc[here, :] = acc[here, :] + prod[base + u]
+            acc[here, :] = acc[here, :] + term
 
 
 def exchange_kernel(n, part_ref, out_ref, parts, send, recv):
@@ -320,7 +317,6 @@
         scratch_shapes=[
             pltpu.VMEM((windows * strike_rows, dip), f32),
             pltpu.VMEM((strike_rows, windows, dip), jnp.bfloat16),
-            pltpu.VMEM((slots, windows, block), f32),
             pltpu.VMEM((row_count + 1, windows, block), f32),
             dma,
             dma((CHUNKS,)),
@@ -357,7 +353,6 @@
         out_specs=(vmem, vmem),
         scratch_shapes=[
             pltpu.VMEM((row_count, windows, block), jnp.bfloat16),
-            pltpu.VMEM((slots, windows, dip), f32),
         ],
         compiler_params=pltpu.CompilerParams(vmem_limit_bytes=VMEM_LIMIT),
         name="adjoint",

time: 47.5 us -> 46.1 us (0.971)
  Pallas kernels: 44.7 us -> 43.4 us
    pallas_call x1, Pallas kernels: 3.7 us -> 2.97 us  [local(): pl.pallas_call(functools.partial(adjoint_kernel, strike_rows), out_shape=...]
    pallas_call x1, Pallas kernels: 7 us -> 6.36 us  [local(): pl.pallas_call(functools.partial(forward_kernel, strike_rows), out_shape=...]
where the time goes in v4:
time: 46.1 us; the launch traced here: 45.9 us
  Pallas kernels  43.4 us (94%)
  other arithmetic  1.19 us (3%)
  between operations  0.69 us (1%)
  local copies, waits for them, and re-layouts  0.66 us (1%)
    pallas_call x1, Pallas kernels, local(): pl.pallas_call(functools.partial(reduce_kernel, n_sta, n_strike), out_sha...  29.3 us
    pallas_call x1, Pallas kernels, local(): pl.pallas_call(functools.partial(forward_kernel, strike_rows), out_shape=...  6.36 us
    pallas_call x1, Pallas kernels, local(): pl.pallas_call(functools.partial(exchange_kernel, n_strike), out_shape=ja...  4.78 us
    pallas_call x1, Pallas kernels, local(): pl.pallas_call(functools.partial(adjoint_kernel, strike_rows), out_shape=...  2.97 us
    sub x1, other arithmetic, local(): updated = model - field.reshape(windows, strike_rows, dip)  1.19 us

profile of v4, /device:TPU:0, one launch (start us, length us, event | category | flops | bytes accessed | tf_op | source)
XLA Modules:
  0.0 45.9 jit_solution(588239910799626924)
XLA Ops:
  0.6 0.0 copy-start
  0.6 0.0 copy-start.1
  0.6 0.7 %copy-done.1 = s32[1,1,96]{2,1,0:T(1,128)S(1)} copy-done((s32[1,1,96]{2,1,0:T(1,128)S(1)}, s32[1,1,96]{2,1,0:T(1,128)}, u32[]{:S(2)}) %copy-start.1) | copy-done | bytes 408
  1.3 6.4 %forward.1 = (f32[8,512]{1,0:T(8,128)S(1)}, bf16[96,128,128]{2,1,0:T(8,128)(2,1)S(1)}) custom-call(s32[96]{0:T(128)S(1)} %bitcast.5, f32[2048,128]{1,0:T(8,128)} %bitcast.7, bf16[96,128,128]{2,1,0:T(8,128)(2,1)} %bitcast.8), custom_call_target="tpu_custom_call" | custom-call | tf_op jit(solution)/shard_map/forward/pallas_call | solution.py:309
  7.7 0.0 copy-start.2
  7.7 4.8 %exchange.1.synth_ref = f32[8,512]{1,0:T(8,128)S(1)} custom-call(f32[8,512]{1,0:T(8,128)S(1)} %get-tuple-element.6.part_ref), custom_call_target="tpu_custom_call" | custom-call | tf_op jit(solution)/shard_map/exchange/pallas_call | solution.py:332
  12.5 0.0 copy-done
  12.5 3.0 %adjoint.1 = (f32[8,512]{1,0:T(8,128)}, f32[2112,128]{1,0:T(8,128)S(1)}) custom-call(s32[96]{0:T(128)S(1)} %bitcast.6, f32[8,512]{1,0:T(8,128)S(1)} %exchange.1.synth_ref, f32[8,512]{1,0:T(8,128)S(1)} %copy-done, bf16[96,128,128]{2,1,0:T(8,128)(2,1)S(1)} %get-tuple-element.7.green_ref), custom_call_target="tpu_custom_call" | custom-call | tf_op jit(solution)/shard_map/adjoint/pallas_call | solution.py:346
  15.4 29.3 %reduce.1 = f32[2,2,4,4,32,128]{5,4,3,2,1,0:T(8,128)S(1)} custom-call(f32[2112,128]{1,0:T(8,128)S(1)} %get-tuple-element.9.acc_ref), custom_call_target="tpu_custom_call" | custom-call | tf_op jit(solution)/shard_map/reduce/pallas_call | solution.py:365
  44.7 0.0 copy-done.2
  44.7 1.2 %bitcast_subtract_fusion = f32[64,32,128]{2,1,0:T(8,128)} fusion(f32[64,32,128]{2,1,0:T(8,128)S(1)} %copy-done.2, f32[2,2,4,4,32,128]{5,4,3,2,1,0:T(8,128)S(1)} %reduce.1), kind=kLoop, calls=%fused_computation | loop fusion | flops 262144 | bytes 3145728 | tf_op jit(solution)/shard_map/sub | solution.py:387
Async XLA Ops:
  0.6 11.8 %copy-start = (f32[8,512]{1,0:T(8,128)S(1)}, f32[8,512]{1,0:T(8,128)}, u32[]{:S(2)}) copy-start(f32[8,512]{1,0:T(8,128)} %data_ref.1) | copy-start | bytes 49156
  0.6 0.7 %copy-start.1 = (s32[1,1,96]{2,1,0:T(1,128)S(1)}, s32[1,1,96]{2,1,0:T(1,128)}, u32[]{:S(2)}) copy-start(s32[1,1,96]{2,1,0:T(1,128)} %param.7) | copy-start | bytes 1156
  7.7 37.0 %copy-start.2 = (f32[64,32,128]{2,1,0:T(8,128)S(1)}, f32[64,32,128]{2,1,0:T(8,128)}, u32[]{:S(2)}) copy-start(f32[64,32,128]{2,1,0:T(8,128)} %param.5) | copy-start | bytes 3145732
